TPU v7x, 512 devices: a whole 4x8x8 slice. The times are simulated.
512 devices in a mesh: ctx: 64 (over x, y_lo, z), fsdp: 8 (over y_hi, core).
Axes of the slice: x: 4, y: 8 (y_hi: 4, y_lo: 2; y = y_hi * 2 + y_lo), z: 8, core: 2. Of those that a mesh axis runs over, the one named last changes fastest.
Arguments:
- queries: bfloat16 [2, 16384, 2048], P(None, 'ctx', 'fsdp'), may hold values from -5.5 to 5.5
- keys_values: bfloat16 [2, 2, 16384, 2048], P(None, None, 'ctx', 'fsdp'), may hold values from -5.5 to 5.5
- block_mask: int32 [256, 32], P('ctx'), may hold values 0 or 1
- out_weight: bfloat16 [2048, 4096], P('fsdp'), may hold values from -3 to 3
Outputs:
- mixed: bfloat16 [2, 16384, 4096], P(None, 'ctx', 'fsdp')
All inputs are finite; a program needn't handle non-finite values. No bound on the sum of `block_mask` on one device may be relied on, other than what follows from the above.
Results may differ from a plain program's by a relative error of at most 0.0058.
Values may be sent and summed in bfloat16 or wider, within the bound.
A program may use at most 64 MiB of HBM per device.

v0:
```python
import math

import jax
import jax.numpy as jnp
from jax import lax
from jax.sharding import PartitionSpec as P

HD = 128
BLK = 64
WINB = 32


def passed_along(array, axis, by):
    devices = lax.axis_size(axis)
    pairs = [(i, i + by) for i in range(devices) if 0 <= i + by < devices]
    return lax.ppermute(array, axis, pairs)


def block_rules(first_block, query_count, key_start, key_count, mask_rows):
    query_blocks = first_block + jnp.arange(query_count, dtype=jnp.int32)
    key_blocks = key_start + jnp.arange(key_count, dtype=jnp.int32)
    block_gap = query_blocks[:, None] - key_blocks[None, :]
    present = key_blocks[None, :] >= 0
    clean_ok = (block_gap >= 0) & (block_gap < WINB) & present
    offsets = jnp.arange(WINB, dtype=jnp.int32)
    picked = ((block_gap - 1)[:, :, None] == offsets[None, None, :]) & (mask_rows[:, None, :] == 1)
    noisy_ok = jnp.any(picked, axis=2) & present
    own_block = query_blocks[:, None] == query_blocks[None, :]

    def widen(table):
        return jnp.repeat(jnp.repeat(table, BLK, axis=0), BLK, axis=1)

    return (widen(clean_ok), widen(noisy_ok), widen(own_block))


def attend(query, keys, values, allowed):
    count, width = query.shape
    heads = width // HD
    query_three = query.reshape(count, heads, HD)
    key_three = keys.reshape(-1, heads, HD)
    value_three = values.reshape(-1, heads, HD)
    scores = jnp.einsum(
        "qhd,khd->hqk", query_three, key_three, preferred_element_type=jnp.float32
    ) * (1.0 / math.sqrt(HD))
    scores = jnp.where(allowed[None], scores, jnp.float32(-1e30))
    top = jnp.max(scores, axis=-1, keepdims=True)
    expo = jnp.exp(scores - top)
    weights = (expo / jnp.sum(expo, axis=-1, keepdims=True)).astype(jnp.bfloat16)
    result = jnp.einsum("hqk,khd->qhd", weights, value_three, preferred_element_type=jnp.float32)
    return result.reshape(count, width).astype(jnp.bfloat16)


def on_device(queries, keys_values, block_mask, out_weight):
    tokens = queries.shape[1]
    blocks_here = tokens // BLK
    reach = WINB * BLK // tokens
    own = keys_values[:, 0]
    pieces = []
    moving = own
    for step in range(reach):
        moving = passed_along(moving, "ctx", 1)
        pieces.insert(0, moving)
    window = jnp.concatenate(pieces + [own], axis=1)
    first_block = lax.axis_index("ctx") * blocks_here
    clean_ok, noisy_ok, own_ok = block_rules(
        first_block, blocks_here, first_block - WINB, blocks_here + WINB, block_mask
    )
    clean_out = attend(queries[0], window[0], window[1], clean_ok)
    noisy_keys = jnp.concatenate([window[0], keys_values[0, 1]], axis=0)
    noisy_values = jnp.concatenate([window[1], keys_values[1, 1]], axis=0)
    noisy_allowed = jnp.concatenate([noisy_ok, own_ok], axis=1)
    noisy_out = attend(queries[1], noisy_keys, noisy_values, noisy_allowed)
    attended = jnp.stack([clean_out, noisy_out])
    panel = lax.all_to_all(out_weight, "fsdp", split_axis=1, concat_axis=0, tiled=True)
    piece = lax.all_gather(attended, "fsdp", axis=2, tiled=True)
    columns = piece.shape[2]
    mixed = jnp.dot(piece.reshape(-1, columns), panel, preferred_element_type=jnp.float32)
    return mixed.astype(jnp.bfloat16).reshape(2, tokens, panel.shape[1])


def solution(mesh):
    in_specs = (
        P(None, "ctx", "fsdp"),
        P(None, None, "ctx", "fsdp"),
        P("ctx", None),
        P("fsdp", None),
    )
    out_specs = P(None, "ctx", "fsdp")
    return jax.shard_map(
        on_device, mesh=mesh, in_specs=in_specs, out_specs=out_specs, check_vma=False
    )
```

profile of v0, /device:TPU:1, one launch (start us, length us, event | category | flops | bytes accessed | tf_op | source)
XLA Modules:
  0.0 229.4 jit_solution(5361212706410624374)
XLA Ops:
  7.6 4.8 %collective-permute-start = (bf16[2,256,256]{1,2,0:T(8,128)(2,1)S(1)}, bf16[2,256,256]{1,2,0:T(8,128)(2,1)S(1)}, u32[]{:S(2)}, u32[]{:S(2)}) collective-permute-start(bf16[2,256,256]{1,2,0:T(8,128)(2,1)S(1)} %bitcast.72), channel_id=1, source_target_pairs={{0,8},{8,16},{16,24},{24,32},{32,40},{40,48},{48,56},{56,64},{64,7... | collective-permute-start | bytes 786440 | tf_op jit(solution)/shard_map/ppermute | solution.py:16
  12.5 3.3 %collective-permute-done = bf16[2,256,256]{1,2,0:T(8,128)(2,1)S(1)} collective-permute-done((bf16[2,256,256]{1,2,0:T(8,128)(2,1)S(1)}, bf16[2,256,256]{1,2,0:T(8,128)(2,1)S(1)}, u32[]{:S(2)}, u32[]{:S(2)}) %collective-permute-start) | collective-permute-done | bytes 262176 | tf_op jit(solution)/shard_map/ppermute | solution.py:16
  15.8 5.7 %collective-permute-start.1 = (bf16[2,256,256]{1,2,0:T(8,128)(2,1)S(1)}, bf16[2,256,256]{1,2,0:T(8,128)(2,1)S(1)}, u32[]{:S(2)}, u32[]{:S(2)}) collective-permute-start(bf16[2,256,256]{1,2,0:T(8,128)(2,1)S(1)} %collective-permute-done), channel_id=1, source_target_pairs={{0,8},{8,16},{16,24},{24,32},{32,40},{40,48},{48,56},{56,64},{64,7... | collective-permute-start | bytes 786440 | tf_op jit(solution)/shard_map/ppermute | solution.py:16
  21.4 3.3 %collective-permute-done.1 = bf16[2,256,256]{1,2,0:T(8,128)(2,1)S(1)} collective-permute-done((bf16[2,256,256]{1,2,0:T(8,128)(2,1)S(1)}, bf16[2,256,256]{1,2,0:T(8,128)(2,1)S(1)}, u32[]{:S(2)}, u32[]{:S(2)}) %collective-permute-start.1) | collective-permute-done | bytes 262176 | tf_op jit(solution)/shard_map/ppermute | solution.py:16
  24.7 5.5 %collective-permute-start.2 = (bf16[2,256,256]{1,2,0:T(8,128)(2,1)S(1)}, bf16[2,256,256]{1,2,0:T(8,128)(2,1)}, u32[]{:S(2)}, u32[]{:S(2)}) collective-permute-start(bf16[2,256,256]{1,2,0:T(8,128)(2,1)S(1)} %collective-permute-done.1), channel_id=1, source_target_pairs={{0,8},{8,16},{16,24},{24,32},{32,40},{40,48},{48,56},{56,64},{64,7... | collective-permute-start | bytes 786440 | tf_op jit(solution)/shard_map/ppermute | solution.py:16
  30.3 4.1 %copy.58 = bf16[256,4096]{0,1:T(8,128)(2,1)} copy(bf16[256,4096]{1,0:T(8,128)(2,1)} %param.7) | data formatting | bytes 4194304 | tf_op args[3]
  34.4 10.1 %all-to-all-start = ((bf16[256,8,512]{0,2,1:T(8,128)(2,1)}), bf16[256,8,512]{0,2,1:T(8,128)(2,1)S(1)}, u32[]{:S(2)}, u32[]{:S(2)}) async-start(bf16[256,8,512]{0,2,1:T(8,128)(2,1)} %bitcast.64), calls=%async_computation | async-start | bytes 4194304 | tf_op jit(solution)/shard_map/all_to_all | solution.py:74
  44.5 4.3 %collective-permute-start.3 = (bf16[2,256,256]{1,2,0:T(8,128)(2,1)}, bf16[2,256,256]{1,2,0:T(8,128)(2,1)S(1)}, u32[]{:S(2)}, u32[]{:S(2)}) collective-permute-start(bf16[2,256,256]{1,2,0:T(8,128)(2,1)} %collective-permute-done.2), channel_id=1, source_target_pairs={{0,8},{8,16},{16,24},{24,32},{32,40},{40,48},{48,56},{56,64},{64,7... | collective-permute-start | bytes 786440 | tf_op jit(solution)/shard_map/ppermute | solution.py:16
  48.9 5.9 %collective-permute-done.3 = bf16[2,256,256]{1,2,0:T(8,128)(2,1)S(1)} collective-permute-done((bf16[2,256,256]{1,2,0:T(8,128)(2,1)}, bf16[2,256,256]{1,2,0:T(8,128)(2,1)S(1)}, u32[]{:S(2)}, u32[]{:S(2)}) %collective-permute-start.3) | collective-permute-done | bytes 262176 | tf_op jit(solution)/shard_map/ppermute | solution.py:16
  54.8 5.3 %collective-permute-start.4 = (bf16[2,256,256]{1,2,0:T(8,128)(2,1)S(1)}, bf16[2,256,256]{1,2,0:T(8,128)(2,1)S(1)}, u32[]{:S(2)}, u32[]{:S(2)}) collective-permute-start(bf16[2,256,256]{1,2,0:T(8,128)(2,1)S(1)} %collective-permute-done.3), channel_id=1, source_target_pairs={{0,8},{8,16},{16,24},{24,32},{32,40},{40,48},{48,56},{56,64},{64,7... | collective-permute-start | bytes 786440 | tf_op jit(solution)/shard_map/ppermute | solution.py:16
  60.2 4.6 %collective-permute-done.4 = bf16[2,256,256]{1,2,0:T(8,128)(2,1)S(1)} collective-permute-done((bf16[2,256,256]{1,2,0:T(8,128)(2,1)S(1)}, bf16[2,256,256]{1,2,0:T(8,128)(2,1)S(1)}, u32[]{:S(2)}, u32[]{:S(2)}) %collective-permute-start.4) | collective-permute-done | bytes 262176 | tf_op jit(solution)/shard_map/ppermute | solution.py:16
  64.8 6.0 %collective-permute-start.5 = (bf16[2,256,256]{1,2,0:T(8,128)(2,1)S(1)}, bf16[2,256,256]{1,2,0:T(8,128)(2,1)}, u32[]{:S(2)}, u32[]{:S(2)}) collective-permute-start(bf16[2,256,256]{1,2,0:T(8,128)(2,1)S(1)} %collective-permute-done.4), channel_id=1, source_target_pairs={{0,8},{8,16},{16,24},{24,32},{32,40},{40,48},{48,56},{56,64},{64,7... | collective-permute-start | bytes 786440 | tf_op jit(solution)/shard_map/ppermute | solution.py:16
  71.0 3.0 %collective-permute-done.5 = bf16[2,256,256]{1,2,0:T(8,128)(2,1)} collective-permute-done((bf16[2,256,256]{1,2,0:T(8,128)(2,1)S(1)}, bf16[2,256,256]{1,2,0:T(8,128)(2,1)}, u32[]{:S(2)}, u32[]{:S(2)}) %collective-permute-start.5) | collective-permute-done | bytes 262176 | tf_op jit(solution)/shard_map/ppermute | solution.py:16
  74.0 4.2 %collective-permute-start.6 = (bf16[2,256,256]{1,2,0:T(8,128)(2,1)}, bf16[2,256,256]{1,2,0:T(8,128)(2,1)S(1)}, u32[]{:S(2)}, u32[]{:S(2)}) collective-permute-start(bf16[2,256,256]{1,2,0:T(8,128)(2,1)} %collective-permute-done.5), channel_id=1, source_target_pairs={{0,8},{8,16},{16,24},{24,32},{32,40},{40,48},{48,56},{56,64},{64,7... | collective-permute-start | bytes 786440 | tf_op jit(solution)/shard_map/ppermute | solution.py:16
  82.9 4.1 %collective-permute-start.7 = (bf16[2,256,256]{1,2,0:T(8,128)(2,1)S(1)}, bf16[2,256,256]{1,2,0:T(8,128)(2,1)S(1)}, u32[]{:S(2)}, u32[]{:S(2)}) collective-permute-start(bf16[2,256,256]{1,2,0:T(8,128)(2,1)S(1)} %collective-permute-done.6), channel_id=1, source_target_pairs={{0,8},{8,16},{16,24},{24,32},{32,40},{40,48},{48,56},{56,64},{64,7... | collective-permute-start | bytes 786440 | tf_op jit(solution)/shard_map/ppermute | solution.py:16
  89.0 1.3 collective-permute-done.7
  93.6 1.4 copy.51
  96.0 2.9 %fusion.58 = f32[2,256]{1,0:T(2,128)S(1)} fusion(bf16[2304,2,128]{0,2,1:T(8,128)(2,1)S(1)} %bitcast.66, bf16[256,2,128]{0,2,1:T(8,128)(2,1)S(1)} %bitcast.77, pred[256,2304]{0,1:T(8,128)(4,1)} %bitcast.73), kind=kOutput, calls=%fused_computation.66 | convolution fusion | flops 306710784 | bytes 1902592 | tf_op jit(solution)/shard_map/sub | solution.py:47
  98.9 4.4 %fusion.15 = bf16[2,128,256]{2,1,0:T(8,128)(2,1)} fusion(bf16[2304,2,128]{0,2,1:T(8,128)(2,1)} %bitcast.70, f32[2,256]{1,0:T(2,128)S(1)} %fusion.58, bf16[2304,2,128]{0,2,1:T(8,128)(2,1)S(1)} %bitcast.67, bf16[256,2,128]{0,2,1:T(8,128)(2,1)S(1)} %bitcast.78, pred[256,2304]{0,1:T(8,128)(4,1)} %bitcast.74), kind=kOutput, calls=%fused_computation.22 | convolution fusion | flops 609946368 | bytes 3213312 | tf_op jit(solution)/shard_map/hqk,khd->qhd/dot_general | solution.py:49
  104.4 3.4 %exponential_reduce_fusion = f32[2,256]{1,0:T(2,128)S(1)} fusion(bf16[256,2,128]{0,2,1:T(8,128)(2,1)} %bitcast.79, pred[256,2560]{0,1:T(8,128)(4,1)} %pad_add_fusion, bf16[256,2,128]{2,0,1:T(8,128)(2,1)S(1)} %copy-done.12, bf16[2304,2,128]{2,0,1:T(8,128)(2,1)} %copy.51), kind=kOutput, calls=%fused_computation.7 | convolution fusion | flops 343411200 | bytes 2099200 | tf_op jit(solution)/shard_map/sub | solution.py:47
  107.8 4.5 %fusion.16 = bf16[2,128,256]{2,1,0:T(8,128)(2,1)} fusion(f32[2,256]{1,0:T(2,128)S(1)} %exponential_reduce_fusion, bf16[256,2,128]{0,2,1:T(8,128)(2,1)} %bitcast.81, bf16[2304,2,128]{0,2,1:T(8,128)(2,1)} %bitcast.71, bf16[256,2,128]{0,2,1:T(8,128)(2,1)} %bitcast.80, pred[256,2560]{0,1:T(8,128)(4,1)} %pad_add_fusion, bf16[256,2,128]{2,0,1:T(8,128)(2,1)S(1)} %copy-done.12, ...), kind=kOutput, calls=%fused_computation.23 | convolution fusion | flops 682953728 | bytes 3540992 | tf_op jit(solution)/shard_map/hqk,khd->qhd/dot_general | solution.py:49
  114.1 2.4 %copy.59 = bf16[8,256,512]{2,1,0:T(8,128)(2,1)} copy(bf16[8,256,512]{1,2,0:T(8,128)(2,1)S(1)} %bitcast.63) | data formatting | bytes 4194304 | tf_op jit(solution)/shard_map/all_to_all | solution.py:74
  116.5 101.8 %all-gather.2.cloned.1.call-done = bf16[2,256,2048]{2,1,0:T(8,128)(2,1)} async-done(((bf16[2,256,256]{2,1,0:T(8,128)(2,1)}), bf16[2,256,2048]{2,1,0:T(8,128)(2,1)}) %all-gather.2.cloned.1.call-update) | async-done | bytes 2097168 | tf_op jit(solution)/shard_map/all_gather | solution.py:75
  218.3 4.3 %convolution_convert_fusion = bf16[512,512]{1,0:T(8,128)(2,1)} fusion(bf16[512,2048]{1,0:T(8,128)(2,1)} %bitcast.84, bf16[2048,512]{1,0:T(8,128)(2,1)} %bitcast.69), kind=kOutput, calls=%fused_computation.21 | convolution fusion | flops 1074003968 | bytes 4718592 | tf_op jit(solution)/shard_map/dot_general | solution.py:77
  (75 shorter events, 15.0 us)
Async XLA Ops:
  7.6 8.1 %collective-permute-start = (bf16[2,256,256]{1,2,0:T(8,128)(2,1)S(1)}, bf16[2,256,256]{1,2,0:T(8,128)(2,1)S(1)}, u32[]{:S(2)}, u32[]{:S(2)}) collective-permute-start(bf16[2,256,256]{1,2,0:T(8,128)(2,1)S(1)} %bitcast.72), channel_id=1, source_target_pairs={{0,8},{8,16},{16,24},{24,32},{32,40},{40,48},{48,56},{56,64},{64,7... | collective-permute-start | bytes 786440 | tf_op jit(solution)/shard_map/ppermute | solution.py:16
  15.8 18.6 %copy-start.3 = (bf16[2,256,256]{1,2,0:T(8,128)(2,1)}, bf16[2,256,256]{1,2,0:T(8,128)(2,1)S(1)}, u32[]{:S(2)}) copy-start(bf16[2,256,256]{1,2,0:T(8,128)(2,1)S(1)} %collective-permute-done) | copy-start | bytes 786436
  15.8 8.9 %collective-permute-start.1 = (bf16[2,256,256]{1,2,0:T(8,128)(2,1)S(1)}, bf16[2,256,256]{1,2,0:T(8,128)(2,1)S(1)}, u32[]{:S(2)}, u32[]{:S(2)}) collective-permute-start(bf16[2,256,256]{1,2,0:T(8,128)(2,1)S(1)} %collective-permute-done), channel_id=1, source_target_pairs={{0,8},{8,16},{16,24},{24,32},{32,40},{40,48},{48,56},{56,64},{64,7... | collective-permute-start | bytes 786440 | tf_op jit(solution)/shard_map/ppermute | solution.py:16
  24.7 9.6 %copy-start.5 = (bf16[2,256,256]{1,2,0:T(8,128)(2,1)}, bf16[2,256,256]{1,2,0:T(8,128)(2,1)S(1)}, u32[]{:S(2)}) copy-start(bf16[2,256,256]{1,2,0:T(8,128)(2,1)S(1)} %collective-permute-done.1) | copy-start | bytes 786436
  24.7 19.7 %collective-permute-start.2 = (bf16[2,256,256]{1,2,0:T(8,128)(2,1)S(1)}, bf16[2,256,256]{1,2,0:T(8,128)(2,1)}, u32[]{:S(2)}, u32[]{:S(2)}) collective-permute-start(bf16[2,256,256]{1,2,0:T(8,128)(2,1)S(1)} %collective-permute-done.1), channel_id=1, source_target_pairs={{0,8},{8,16},{16,24},{24,32},{32,40},{40,48},{48,56},{56,64},{64,7... | collective-permute-start | bytes 786440 | tf_op jit(solution)/shard_map/ppermute | solution.py:16
  34.3 25.8 %copy-start.13 = (s32[4,32]{1,0:T(4,128)S(1)}, s32[4,32]{1,0:T(4,128)}, u32[]{:S(2)}) copy-start(s32[4,32]{1,0:T(4,128)} %param.6) | copy-start | bytes 1540
  34.3 36.6 %copy-start.2 = (bf16[2,256,256]{2,1,0:T(8,128)(2,1)S(1)}, bf16[2,256,256]{2,1,0:T(8,128)(2,1)}, u32[]{:S(2)}) copy-start(bf16[2,256,256]{2,1,0:T(8,128)(2,1)} %param.4) | copy-start | bytes 786436
  34.3 46.1 %copy-start.1 = (bf16[2,2,256,256]{3,2,1,0:T(8,128)(2,1)S(1)}, bf16[2,2,256,256]{3,2,1,0:T(8,128)(2,1)}, u32[]{:S(2)}) copy-start(bf16[2,2,256,256]{3,2,1,0:T(8,128)(2,1)} %param.5) | copy-start | bytes 1572868
  34.4 79.7 %all-to-all-start = ((bf16[256,8,512]{0,2,1:T(8,128)(2,1)}), bf16[256,8,512]{0,2,1:T(8,128)(2,1)S(1)}, u32[]{:S(2)}, u32[]{:S(2)}) async-start(bf16[256,8,512]{0,2,1:T(8,128)(2,1)} %bitcast.64), calls=%async_computation | async-start | bytes 4194304 | tf_op jit(solution)/shard_map/all_to_all | solution.py:74
  44.5 173.8 %all-gather.2.cloned.1.call-start = ((), (), s32[]{:S(2)}) async-start(), calls=%async_computation.1 | async-start | bytes 2359296 | tf_op jit(solution)/shard_map/all_gather | solution.py:75
  44.5 10.3 %collective-permute-start.3 = (bf16[2,256,256]{1,2,0:T(8,128)(2,1)}, bf16[2,256,256]{1,2,0:T(8,128)(2,1)S(1)}, u32[]{:S(2)}, u32[]{:S(2)}) collective-permute-start(bf16[2,256,256]{1,2,0:T(8,128)(2,1)} %collective-permute-done.2), channel_id=1, source_target_pairs={{0,8},{8,16},{16,24},{24,32},{32,40},{40,48},{48,56},{56,64},{64,7... | collective-permute-start | bytes 786440 | tf_op jit(solution)/shard_map/ppermute | solution.py:16
  54.8 16.1 %copy-start.7 = (bf16[2,256,256]{1,2,0:T(8,128)(2,1)}, bf16[2,256,256]{1,2,0:T(8,128)(2,1)S(1)}, u32[]{:S(2)}) copy-start(bf16[2,256,256]{1,2,0:T(8,128)(2,1)S(1)} %collective-permute-done.3) | copy-start | bytes 786436
  54.8 10.1 %collective-permute-start.4 = (bf16[2,256,256]{1,2,0:T(8,128)(2,1)S(1)}, bf16[2,256,256]{1,2,0:T(8,128)(2,1)S(1)}, u32[]{:S(2)}, u32[]{:S(2)}) collective-permute-start(bf16[2,256,256]{1,2,0:T(8,128)(2,1)S(1)} %collective-permute-done.3), channel_id=1, source_target_pairs={{0,8},{8,16},{16,24},{24,32},{32,40},{40,48},{48,56},{56,64},{64,7... | collective-permute-start | bytes 786440 | tf_op jit(solution)/shard_map/ppermute | solution.py:16
  64.8 6.1 %copy-start.9 = (bf16[2,256,256]{1,2,0:T(8,128)(2,1)}, bf16[2,256,256]{1,2,0:T(8,128)(2,1)S(1)}, u32[]{:S(2)}) copy-start(bf16[2,256,256]{1,2,0:T(8,128)(2,1)S(1)} %collective-permute-done.4) | copy-start | bytes 786436
  64.8 9.2 %collective-permute-start.5 = (bf16[2,256,256]{1,2,0:T(8,128)(2,1)S(1)}, bf16[2,256,256]{1,2,0:T(8,128)(2,1)}, u32[]{:S(2)}, u32[]{:S(2)}) collective-permute-start(bf16[2,256,256]{1,2,0:T(8,128)(2,1)S(1)} %collective-permute-done.4), channel_id=1, source_target_pairs={{0,8},{8,16},{16,24},{24,32},{32,40},{40,48},{48,56},{56,64},{64,7... | collective-permute-start | bytes 786440 | tf_op jit(solution)/shard_map/ppermute | solution.py:16
  74.0 8.9 %collective-permute-start.6 = (bf16[2,256,256]{1,2,0:T(8,128)(2,1)}, bf16[2,256,256]{1,2,0:T(8,128)(2,1)S(1)}, u32[]{:S(2)}, u32[]{:S(2)}) collective-permute-start(bf16[2,256,256]{1,2,0:T(8,128)(2,1)} %collective-permute-done.5), channel_id=1, source_target_pairs={{0,8},{8,16},{16,24},{24,32},{32,40},{40,48},{48,56},{56,64},{64,7... | collective-permute-start | bytes 786440 | tf_op jit(solution)/shard_map/ppermute | solution.py:16
  80.5 10.8 %copy-start.10 = (bf16[2,256,256]{1,2,0:T(8,128)(2,1)S(1)}, bf16[2,256,256]{1,2,0:T(8,128)(2,1)}, u32[]{:S(2)}) copy-start(bf16[2,256,256]{1,2,0:T(8,128)(2,1)} %copy-done.9) | copy-start | bytes 786436
  81.4 10.0 %copy-start.8 = (bf16[2,256,256]{1,2,0:T(8,128)(2,1)S(1)}, bf16[2,256,256]{1,2,0:T(8,128)(2,1)}, u32[]{:S(2)}) copy-start(bf16[2,256,256]{1,2,0:T(8,128)(2,1)} %copy-done.7) | copy-start | bytes 786436
  82.9 7.4 %collective-permute-start.7 = (bf16[2,256,256]{1,2,0:T(8,128)(2,1)S(1)}, bf16[2,256,256]{1,2,0:T(8,128)(2,1)S(1)}, u32[]{:S(2)}, u32[]{:S(2)}) collective-permute-start(bf16[2,256,256]{1,2,0:T(8,128)(2,1)S(1)} %collective-permute-done.6), channel_id=1, source_target_pairs={{0,8},{8,16},{16,24},{24,32},{32,40},{40,48},{48,56},{56,64},{64,7... | collective-permute-start | bytes 786440 | tf_op jit(solution)/shard_map/ppermute | solution.py:16
  87.9 4.5 %copy-start.6 = (bf16[2,256,256]{1,2,0:T(8,128)(2,1)S(1)}, bf16[2,256,256]{1,2,0:T(8,128)(2,1)}, u32[]{:S(2)}) copy-start(bf16[2,256,256]{1,2,0:T(8,128)(2,1)} %copy-done.5) | copy-start | bytes 786436
  87.9 4.5 %copy-start.4 = (bf16[2,256,256]{1,2,0:T(8,128)(2,1)S(1)}, bf16[2,256,256]{1,2,0:T(8,128)(2,1)}, u32[]{:S(2)}) copy-start(bf16[2,256,256]{1,2,0:T(8,128)(2,1)} %copy-done.3) | copy-start | bytes 786436
  93.6 2.4 %copy-start.11 = (bf16[1,256,256]{1,2,0:T(8,128)(2,1)S(1)}, bf16[1,256,256]{1,2,0:T(8,128)(2,1)}, u32[]{:S(2)}) copy-start(bf16[1,256,256]{1,2,0:T(8,128)(2,1)} %copy.66) | copy-start | bytes 393220
  98.9 5.4 %copy-start.12 = (bf16[256,2,128]{2,0,1:T(8,128)(2,1)S(1)}, bf16[256,2,128]{2,0,1:T(8,128)(2,1)}, u32[]{:S(2)}) copy-start(bf16[256,2,128]{2,0,1:T(8,128)(2,1)} %copy.52) | copy-start | bytes 393220
  104.4 3.4 %copy-start = (bf16[2304,2,128]{2,0,1:T(8,128)(2,1)S(1)}, bf16[2304,2,128]{2,0,1:T(8,128)(2,1)}, u32[]{:S(2)}) copy-start(bf16[2304,2,128]{2,0,1:T(8,128)(2,1)} %copy.51) | copy-start | bytes 3538948
Sparse Core Ops, SparseCore 0:
  114.2 104.0 all-gather.1
where the time goes:
time: 230 us; the launch traced here: 229 us
  waiting for transfers between devices  123 us (53%)
  starting transfers between devices  50.1 us (22%)
  local copies, waits for them, and re-layouts  20.7 us (9%)
  matrix products  19.5 us (8%)
  between operations  13.7 us (6%)
    all_gather x1, waiting for transfers between devices, on_device(): piece = lax.all_gather(attended, 'fsdp', axis=2, tiled=True)  102 us
    ppermute x8, starting transfers between devices, passed_along(): return lax.ppermute(array, axis, pairs)  40 us
    ppermute x8, waiting for transfers between devices, passed_along(): return lax.ppermute(array, axis, pairs)  21.4 us
    all_to_all x1, starting transfers between devices, on_device(): lax.all_to_all(out_weight, 'fsdp', split_axis=1, concat_axis=0, tiled=True)  10.1 us
    dot_general x2, matrix products, attend(): jnp.einsum('hqk,khd->qhd', weights, value_three, preferred_element_type=j...  8.93 us
    unnamed x41, local copies, waits for them, and re-layouts  7.94 us
    sub x2, matrix products, attend(): expo = jnp.exp(scores - top)  6.32 us
  transfers between devices with their start and end apart: 10, of which 7 were waited for; matrix products, arithmetic and copies ran while one was open for 16% of the time, Pallas kernels for 0%

commit v1 on v0

v1 whole, which is shorter than its diff:
```python
import functools
import math

import jax
import jax.numpy as jnp
from jax import lax
from jax.experimental import pallas as pl
from jax.experimental.pallas import tpu as pltpu
from jax.sharding import PartitionSpec as P

HD = 128
BLK = 64
WINB = 32
NX, NL, NZ, NH, NC = 4, 2, 8, 4, 2
NCTX = NX * NL * NZ
ROW = NZ
TOK = 256
BLOCKS = TOK // BLK
HEADS = 2
FEAT = 512
NEG = -1e30
EXP_SCALE = math.log2(math.e) / math.sqrt(HD)


def mod(value, size):
    return lax.rem(value + 2 * size, size)


def kernel(
    mask_ref, q_hbm, kv_hbm, w_hbm, out_ref,
    qbuf, kvbuf, win, bias, top, acc, att, panel, total,
    local_sem, kv_send, kv_recv, ag_send, ag_recv, sib_send, sib_recv,
    wy_send, wy_recv, ws_send, ws_recv, wx_send, wx_recv,
):
    ctx = lax.axis_index("ctx")
    fsdp = lax.axis_index("fsdp")
    x = ctx // (NL * NZ)
    low = lax.rem(ctx // NZ, NL)
    z = lax.rem(ctx, NZ)
    high = fsdp // NC
    core = lax.rem(fsdp, NC)

    def along(by):
        return (mod(ctx + by, NCTX), fsdp)

    def at_high(h, l, c):
        return ((x * NL + l) * NZ + z, h * NC + c)

    def at_x(by):
        return (mod(x + by, NX) * (NL * NZ) + lax.rem(ctx, NL * NZ), fsdp)

    h_up, h_down, h_far = mod(high + 1, NH), mod(high - 1, NH), mod(high + 2, NH)
    sibling = (ctx, high * NC + (1 - core))

    load_kv = pltpu.make_async_copy(kv_hbm, kvbuf, local_sem.at[0])
    load_q = pltpu.make_async_copy(q_hbm, qbuf, local_sem.at[1])
    load_w = pltpu.make_async_copy(
        w_hbm.at[:, :, :, pl.ds(pl.multiple_of(fsdp * FEAT, FEAT), FEAT)],
        panel.at[0, :, core],
        local_sem.at[2],
    )
    load_kv.start()
    load_q.start()
    load_w.start()

    barrier = pltpu.get_barrier_semaphore()
    sources = [along(-1), along(1), along(-ROW)]
    sources += [at_high(h_up, low, core), at_high(h_down, low, core), sibling]
    for c in range(NC):
        sources += [at_high(h_up, 0, c), at_high(h_down, 1, c), at_high(h_far, 1 - low, c)]
    sources += [at_x(1), at_x(-1)]
    for device in sources:
        pl.semaphore_signal(barrier, inc=1, device_id=device, device_id_type=pl.DeviceIdType.MESH)
    pl.semaphore_wait(barrier, len(sources))

    def remote(src, dst, send, recv, device):
        return pltpu.make_async_remote_copy(
            src_ref=src, dst_ref=dst, send_sem=send, recv_sem=recv,
            device_id=device, device_id_type=pl.DeviceIdType.MESH,
        )

    def own(hd, kv):
        return kvbuf.at[kv, 0, :, hd * HD:(hd + 1) * HD]

    def kv_copy(hd, slot, kv):
        forward = slot < 4 or (slot == 4 and kv == 0)
        if forward:
            src = own(hd, kv) if slot == 1 else win.at[hd, slot - 2, kv]
            device = along(1)
        elif slot == 8:
            src, device = own(hd, kv), along(ROW)
        else:
            src, device = win.at[hd, slot, kv], along(-1)
        return remote(src, win.at[hd, slot - 1, kv], kv_send.at[hd, slot - 1, kv],
                      kv_recv.at[hd, slot - 1, kv], device)

    def start_kv(hd):
        for kv in range(2):
            kv_copy(hd, 1, kv).start()
            kv_copy(hd, 8, kv).start()

    load_kv.wait()
    start_kv(0)

    half, part = x // 2, lax.rem(x, 2)
    sign = 2 * low - 1
    w_targets = [
        (mod(high + sign, NH), 0, mod(-sign, NH)),
        (mod(high + sign, NH), 1, mod(-sign, NH)),
        (h_far, 1 - low, 2),
    ]
    w_copies = []
    for n, (h, l, k) in enumerate(w_targets):
        for c in range(NC):
            cols = pl.ds(pl.multiple_of((h * NC + c) * FEAT, FEAT), FEAT)
            w_copies.append(remote(
                w_hbm.at[half, part, :, cols], panel.at[k, half, core, part],
                wy_send.at[n, c], wy_recv, at_high(h, l, c),
            ))
    other = high * NC + (1 - core)
    w_sib = remote(
        w_hbm.at[:, :, :, pl.ds(pl.multiple_of(other * FEAT, FEAT), FEAT)],
        panel.at[0, :, core], ws_send, ws_recv, sibling,
    )
    for copy in w_copies:
        copy.start()
    w_sib.start()

    def w_quarter(by):
        xx = mod(x + by, NX)
        return panel.at[1:4, xx // 2, :, lax.rem(xx, 2)]

    def w_half(by, c):
        xx = mod(x + by, NX)
        return panel.at[1:4, xx // 2, c, lax.rem(xx, 2)]

    def await_bytes(ref, sem):
        pltpu.make_async_copy(ref, ref, sem).wait()

    wx_copies = [
        remote(w_quarter(0), w_quarter(0), wx_send.at[0], wx_recv.at[0], at_x(1)),
        remote(w_quarter(0), w_quarter(0), wx_send.at[1], wx_recv.at[1], at_x(-1)),
        remote(w_half(-1, 0), w_half(-1, 0), wx_send.at[2], wx_recv.at[2], at_x(1)),
        remote(w_half(1, 1), w_half(1, 1), wx_send.at[3], wx_recv.at[3], at_x(-1)),
    ]

    def w_stage_1():
        await_bytes(w_quarter(0), wy_recv)
        wx_copies[0].start()
        wx_copies[1].start()

    def w_stage_2():
        await_bytes(w_quarter(-1), wx_recv.at[0])
        wx_copies[2].start()
        await_bytes(w_quarter(1), wx_recv.at[1])
        wx_copies[3].start()

    lane_block = lax.broadcasted_iota(jnp.int32, (8, TOK), 1) // BLK
    for slot in range(9):
        here = ctx >= slot
        for a in range(BLOCKS):
            clean = jnp.zeros((8, TOK), jnp.int32)
            noisy = jnp.zeros((8, TOK), jnp.int32)
            for b in range(BLOCKS):
                gap = 4 * slot + a - b
                is_b = lane_block == b
                if 0 <= gap < WINB:
                    clean = jnp.where(is_b, 1, clean)
                if 1 <= gap <= WINB:
                    noisy = jnp.where(is_b, mask_ref[a, gap - 1], noisy)
            present = jnp.where(here, 1, 0)
            bias[0, slot, a] = jnp.where(clean * present == 1, 0.0, NEG)
            bias[1, slot, a] = jnp.where(noisy * present == 1, 0.0, NEG)
    for a in range(BLOCKS):
        bias[1, 9, a] = jnp.where(lane_block == a, 0.0, NEG)

    ones = jnp.ones((TOK, HD), jnp.bfloat16)

    def attend(hd, copy, chunks, first):
        q = qbuf[copy, :, hd * HD:(hd + 1) * HD]
        scores = []
        for keys, _, slot in chunks:
            s = lax.dot_general(
                q, keys, (((1,), (1,)), ((), ())), preferred_element_type=jnp.float32
            )
            s = s.reshape(BLOCKS, BLK // 8, 8, TOK) + bias[copy, slot][:, None]
            scores.append(s.reshape(TOK, TOK))
        best = scores[0]
        for s in scores[1:]:
            best = jnp.maximum(best, s)
        best = jnp.max(best, axis=1, keepdims=True)
        if first:
            new_top = jnp.broadcast_to(best, (TOK, HD))
        else:
            old_top = top[copy]
            new_top = jnp.maximum(old_top, best)
        wide = jnp.concatenate([new_top, new_top], axis=1)
        gained = None
        for s, (_, values, _) in zip(scores, chunks):
            p = jnp.exp2((s - wide) * EXP_SCALE).astype(jnp.bfloat16)
            term = jnp.dot(
                p, jnp.concatenate([values, ones], axis=1), preferred_element_type=jnp.float32
            )
            gained = term if gained is None else gained + term
        if not first:
            fade = jnp.exp2((old_top - new_top) * EXP_SCALE)
            gained = gained + acc[copy] * jnp.concatenate([fade, fade], axis=1)
        acc[copy] = gained
        top[copy] = new_top

    def finish(hd, copy):
        both = acc[copy]
        att[hd, copy, 0, core] = (both[:, :HD] / both[:, HD:]).astype(jnp.bfloat16)

    def ag_up(hd, copy):
        return remote(att.at[hd, copy, 0, core], att.at[hd, copy, 3, core],
                      ag_send.at[hd, copy, 0], ag_recv.at[hd, copy, 2], at_high(h_up, low, core))

    def ag_down(hd, copy):
        return remote(att.at[hd, copy, 0, core], att.at[hd, copy, 1, core],
                      ag_send.at[hd, copy, 1], ag_recv.at[hd, copy, 0], at_high(h_down, low, core))

    def ag_far(hd, copy):
        slot = 3 if copy == 0 else 1
        to = h_up if copy == 0 else h_down
        return remote(att.at[hd, copy, slot, core], att.at[hd, copy, 2, core],
                      ag_send.at[hd, copy, 2], ag_recv.at[hd, copy, 1], at_high(to, low, core))

    def ag_sib(hd, copy, slot):
        return remote(att.at[hd, copy, slot, core], att.at[hd, copy, slot, core],
                      sib_send.at[hd, copy, slot], sib_recv.at[hd, copy, slot], sibling)

    def gather_start(hd, copy):
        ag_up(hd, copy).start()
        ag_down(hd, copy).start()
        ag_sib(hd, copy, 0).start()

    def gather_near(hd):
        for copy in range(2):
            order = (3, 1) if copy == 0 else (1, 3)
            for slot in order:
                if slot == 3:
                    ag_up(hd, copy).wait_recv()
                else:
                    ag_down(hd, copy).wait_recv()
                if slot == order[0]:
                    ag_far(hd, copy).start()
                ag_sib(hd, copy, slot).start()

    def gather_far(hd):
        for copy in range(2):
            ag_far(hd, copy).wait_recv()
            ag_sib(hd, copy, 2).start()

    def own_step(hd):
        keys, values = own(hd, 0)[...], own(hd, 1)[...]
        late_keys = kvbuf[0, 1, :, hd * HD:(hd + 1) * HD]
        late_values = kvbuf[1, 1, :, hd * HD:(hd + 1) * HD]
        attend(hd, 0, [(keys, values, 0)], True)
        attend(hd, 1, [(keys, values, 0), (late_keys, late_values, 9)], True)

    def pair_compute(hd, near, far, copy):
        chunks = [(win[hd, s - 1, 0], win[hd, s - 1, 1], s) for s in (near, far)]
        attend(hd, copy, chunks, False)

    load_q.wait()
    for hd in range(HEADS):
        own_step(hd)
        for step in (1, 2, 3, 4):
            near, far = step, 9 - step
            if step < 4:
                for kv in range(2):
                    kv_copy(hd, near, kv).wait_recv()
                    if step < 3 or kv == 0:
                        kv_copy(hd, near + 1, kv).start()
                    kv_copy(hd, far, kv).wait_recv()
                    kv_copy(hd, far - 1, kv).start()
            else:
                kv_copy(hd, 5, 1).wait_recv()
                kv_copy(hd, 4, 1).start()
                kv_copy(hd, 5, 0).wait_recv()
                if hd == 0:
                    start_kv(1)
                kv_copy(hd, 4, 0).wait_recv()
                kv_copy(hd, 4, 1).wait_recv()
            for copy in range(2):
                pair_compute(hd, near, far, copy)
                if step == 4:
                    finish(hd, copy)
                    gather_start(hd, copy)
            if hd == 0 and step == 4:
                w_stage_1()
            if hd == 1 and step == 2:
                w_stage_2()
            if hd == 1 and step == 3:
                gather_near(0)

    gather_far(0)

    def project(hd, copy, k):
        rows = jnp.concatenate([att[hd, copy, k, 0], att[hd, copy, k, 1]], axis=1)
        weight = panel[k, hd].reshape(2 * HD, FEAT)
        return jnp.dot(rows, weight, preferred_element_type=jnp.float32)

    load_w.wait()
    await_bytes(panel.at[0, :, 1 - core], ws_recv)
    await_bytes(w_half(2, 0), wx_recv.at[2])
    await_bytes(w_half(2, 1), wx_recv.at[3])
    for k in (0, 1, 3, 2):
        for copy in range(2):
            ag_sib(0, copy, k).wait_recv()
            term = project(0, copy, k)
            total[copy] = term if k == 0 else total[copy] + term
    gather_near(1)
    for copy in range(2):
        ag_sib(1, copy, 0).wait_recv()
        total[copy] = total[copy] + project(1, copy, 0)
    for copy in range(2):
        for k in (1, 3):
            ag_sib(1, copy, k).wait_recv()
            total[copy] = total[copy] + project(1, copy, k)
    gather_far(1)
    for copy in range(2):
        ag_sib(1, copy, 2).wait_recv()
        out_ref[copy] = (total[copy] + project(1, copy, 2)).astype(jnp.bfloat16)

    for hd in range(HEADS):
        for slot in range(1, 9):
            for kv in range(2):
                kv_copy(hd, slot, kv).wait_send()
        for copy in range(2):
            ag_up(hd, copy).wait_send()
            ag_down(hd, copy).wait_send()
            ag_far(hd, copy).wait_send()
            for slot in range(4):
                ag_sib(hd, copy, slot).wait_send()
    for copy in w_copies:
        copy.wait_send()
    w_sib.wait_send()
    for copy in wx_copies:
        copy.wait_send()


def on_device(queries, keys_values, block_mask, out_weight):
    weight = out_weight.reshape(HEADS, 2, HD // 2, out_weight.shape[1])
    dma = pltpu.SemaphoreType.DMA
    return pl.pallas_call(
        kernel,
        out_shape=jax.ShapeDtypeStruct((2, TOK, FEAT), jnp.bfloat16),
        in_specs=[
            pl.BlockSpec(memory_space=pltpu.SMEM),
            pl.BlockSpec(memory_space=pl.ANY),
            pl.BlockSpec(memory_space=pl.ANY),
            pl.BlockSpec(memory_space=pl.ANY),
        ],
        out_specs=pl.BlockSpec(memory_space=pltpu.VMEM),
        scratch_shapes=[
            pltpu.VMEM((2, TOK, HEADS * HD), jnp.bfloat16),
            pltpu.VMEM((2, 2, TOK, HEADS * HD), jnp.bfloat16),
            pltpu.VMEM((HEADS, 8, 2, TOK, HD), jnp.bfloat16),
            pltpu.VMEM((2, 10, BLOCKS, 8, TOK), jnp.float32),
            pltpu.VMEM((2, TOK, HD), jnp.float32),
            pltpu.VMEM((2, TOK, 2 * HD), jnp.float32),
            pltpu.VMEM((HEADS, 2, NH, NC, TOK, HD), jnp.bfloat16),
            pltpu.VMEM((NH, HEADS, NC, 2, HD // 2, FEAT), jnp.bfloat16),
            pltpu.VMEM((2, TOK, FEAT), jnp.float32),
            dma((3,)),
            dma((HEADS, 8, 2)),
            dma((HEADS, 8, 2)),
            dma((HEADS, 2, 3)),
            dma((HEADS, 2, 3)),
            dma((HEADS, 2, 4)),
            dma((HEADS, 2, 4)),
            dma((3, NC)),
            dma,
            dma,
            dma,
            dma((4,)),
            dma((4,)),
        ],
        compiler_params=pltpu.CompilerParams(
            collective_id=0, has_side_effects=True, vmem_limit_bytes=40 * 1024 * 1024
        ),
    )(block_mask, queries, keys_values, weight)


def solution(mesh):
    in_specs = (
        P(None, "ctx", "fsdp"),
        P(None, None, "ctx", "fsdp"),
        P("ctx", None),
        P("fsdp", None),
    )
    out_specs = P(None, "ctx", "fsdp")
    return jax.shard_map(
        on_device, mesh=mesh, in_specs=in_specs, out_specs=out_specs, check_vma=False
    )
```

time: 230 us -> 87.4 us (0.38)
  waiting for transfers between devices: 123 us -> 0 us
  Pallas kernels: 0 us -> 82.1 us
  starting transfers between devices: 50.1 us -> 0 us
  matrix products: 19.5 us -> 0 us
  local copies, waits for them, and re-layouts: 20.7 us -> 5.06 us
  between operations: 13.7 us -> 0.01 us
    all_gather x1 -> x0, waiting for transfers between devices: 102 us -> none  [on_device(): piece = lax.all_gather(attended, 'fsdp', axis=2, tiled=True)]
    pallas_call x0 -> x1, Pallas kernels: none -> 82.1 us  [on_device(): pl.pallas_call(kernel, out_shape=jax.ShapeDtypeStruct((2, TOK, FEAT), jnp...]
    ppermute x8 -> x0, starting transfers between devices: 40 us -> none  [passed_along(): return lax.ppermute(array, axis, pairs)]
    ppermute x8 -> x0, waiting for transfers between devices: 21.4 us -> none  [passed_along(): return lax.ppermute(array, axis, pairs)]
    dot_general x3 -> x0, matrix products: 13.2 us -> none  [the longest x2 8.93 us: attend(): jnp.einsum('hqk,khd->qhd', weights, value_three, preferred_element_type=j...]
    all_to_all x1 -> x0, starting transfers between devices: 10.1 us -> none  [on_device(): lax.all_to_all(out_weight, 'fsdp', split_axis=1, concat_axis=0, tiled=True)]
    sub x2 -> x0, matrix products: 6.32 us -> none  [attend(): expo = jnp.exp(scores - top)]
    slice x5 -> x0, local copies, waits for them, and re-layouts: 2.93 us -> none  [the longest x2 1.18 us: on_device(): clean_out = attend(queries[0], window[0], window[1], clean_ok)]
  transfers between devices with their start and end apart: 10 -> 0, of which waited for: 7 -> 0; matrix products, arithmetic and copies ran while one was open for 16% -> 0% of each run, Pallas kernels for 0% -> 0%
where the time goes in v1:
time: 87.4 us; the launch traced here: 87.2 us
  Pallas kernels  82.1 us (94%)
  local copies, waits for them, and re-layouts  5.06 us (6%)
    pallas_call x1, Pallas kernels, on_device(): pl.pallas_call(kernel, out_shape=jax.ShapeDtypeStruct((2, TOK, FEAT), jnp...  82.1 us
    unnamed x9, local copies, waits for them, and re-layouts  5.06 us

profile of v1, /device:TPU:1, one launch (start us, length us, event | category | flops | bytes accessed | tf_op | source)
XLA Modules:
  0.0 87.2 jit_solution(4777200511276971585)
XLA Ops:
  0.0 0.0 copy-start
  0.0 1.6 %copy-done = bf16[256,4096]{1,0:T(8,128)(2,1)S(1)} copy-done((bf16[256,4096]{1,0:T(8,128)(2,1)S(1)}, bf16[256,4096]{1,0:T(8,128)(2,1)}, u32[]{:S(2)}) %copy-start) | copy-done | bytes 2097176
  1.6 0.0 copy-start.1
  1.6 1.0 %copy-done.1 = bf16[2,2,256,256]{3,2,1,0:T(8,128)(2,1)S(1)} copy-done((bf16[2,2,256,256]{3,2,1,0:T(8,128)(2,1)S(1)}, bf16[2,2,256,256]{3,2,1,0:T(8,128)(2,1)}, u32[]{:S(2)}) %copy-start.1) | copy-done | bytes 524312
  2.6 0.0 copy-start.2
  2.6 0.9 %copy-done.2 = bf16[2,256,256]{2,1,0:T(8,128)(2,1)S(1)} copy-done((bf16[2,256,256]{2,1,0:T(8,128)(2,1)S(1)}, bf16[2,256,256]{2,1,0:T(8,128)(2,1)}, u32[]{:S(2)}) %copy-start.2) | copy-done | bytes 262168
  3.6 0.0 copy-start.3
  3.6 0.7 copy-done.3
  4.3 82.1 %shard_map.46 = bf16[2,256,512]{2,1,0:T(8,128)(2,1)S(1)} custom-call(s32[4,32]{1,0:T(4,128)S(1)} %copy-done.3, bf16[2,256,256]{2,1,0:T(8,128)(2,1)S(1)} %copy-done.2, bf16[2,2,256,256]{3,2,1,0:T(8,128)(2,1)S(1)} %copy-done.1, bf16[2,2,64,4096]{3,2,1,0:T(8,128)(2,1)S(1)} %bitcast.1), custom_call_target="tpu_custom_call" | custom-call | tf_op jit(solution)/shard_map/pallas_call | solution.py:347
  86.4 0.8 copy.6
Async XLA Ops:
  0.0 1.6 %copy-start = (bf16[256,4096]{1,0:T(8,128)(2,1)S(1)}, bf16[256,4096]{1,0:T(8,128)(2,1)}, u32[]{:S(2)}) copy-start(bf16[256,4096]{1,0:T(8,128)(2,1)} %param.7) | copy-start | bytes 6291460
  1.6 1.0 %copy-start.1 = (bf16[2,2,256,256]{3,2,1,0:T(8,128)(2,1)S(1)}, bf16[2,2,256,256]{3,2,1,0:T(8,128)(2,1)}, u32[]{:S(2)}) copy-start(bf16[2,2,256,256]{3,2,1,0:T(8,128)(2,1)} %kv_hbm.1) | copy-start | bytes 1572868
  2.6 0.9 %copy-start.2 = (bf16[2,256,256]{2,1,0:T(8,128)(2,1)S(1)}, bf16[2,256,256]{2,1,0:T(8,128)(2,1)}, u32[]{:S(2)}) copy-start(bf16[2,256,256]{2,1,0:T(8,128)(2,1)} %q_hbm.1) | copy-start | bytes 786436
  3.6 0.7 copy-start.3

commit v2 on v1

v2 whole, which is shorter than its diff:
```python
import functools
import math

import jax
import jax.numpy as jnp
from jax import lax
from jax.experimental import pallas as pl
from jax.experimental.pallas import tpu as pltpu
from jax.sharding import PartitionSpec as P

HD = 128
BLK = 64
WINB = 32
NX, NL, NZ, NH, NC = 4, 2, 8, 4, 2
NCTX = NX * NL * NZ
ROW = NZ
TOK = 256
BLOCKS = TOK // BLK
HEADS = 2
FEAT = 512
NEG = -1e30
EXP_SCALE = math.log2(math.e) / math.sqrt(HD)


def mod(value, size):
    return lax.rem(value + 2 * size, size)


def kernel(
    mask_ref, q_hbm, kv_hbm, w_hbm, out_ref,
    qbuf, kvbuf, win, bias, top, acc, att, panel, total,
    local_sem, kv_send, kv_recv, ag_send, ag_recv, sib_send, sib_recv,
    wy_send, wy_recv, ws_send, ws_recv, wx_send, wx_recv,
):
    ctx = lax.axis_index("ctx")
    fsdp = lax.axis_index("fsdp")
    x = ctx // (NL * NZ)
    low = lax.rem(ctx // NZ, NL)
    z = lax.rem(ctx, NZ)
    high = fsdp // NC
    core = lax.rem(fsdp, NC)

    def along(by):
        return (mod(ctx + by, NCTX), fsdp)

    def at_high(h, l, c):
        return ((x * NL + l) * NZ + z, h * NC + c)

    def at_x(by):
        return (mod(x + by, NX) * (NL * NZ) + lax.rem(ctx, NL * NZ), fsdp)

    h_up, h_down, h_far = mod(high + 1, NH), mod(high - 1, NH), mod(high + 2, NH)
    sibling = (ctx, high * NC + (1 - core))

    load_kv = pltpu.make_async_copy(kv_hbm, kvbuf, local_sem.at[0])
    load_q = pltpu.make_async_copy(q_hbm, qbuf, local_sem.at[1])
    load_w = pltpu.make_async_copy(
        w_hbm.at[:, :, :, pl.ds(pl.multiple_of(fsdp * FEAT, FEAT), FEAT)],
        panel.at[0, :, core],
        local_sem.at[2],
    )
    load_kv.start()
    load_q.start()
    load_w.start()

    barrier = pltpu.get_barrier_semaphore()
    sources = [along(-1), along(1), along(-ROW)]
    sources += [at_high(h_up, low, core), at_high(h_down, low, core), sibling]
    for c in range(NC):
        sources += [at_high(h_up, 0, c), at_high(h_down, 1, c), at_high(h_far, 1 - low, c)]
    sources += [at_x(1), at_x(-1)]
    for device in sources:
        pl.semaphore_signal(barrier, inc=1, device_id=device, device_id_type=pl.DeviceIdType.MESH)
    pl.semaphore_wait(barrier, len(sources))

    def remote(src, dst, send, recv, device):
        return pltpu.make_async_remote_copy(
            src_ref=src, dst_ref=dst, send_sem=send, recv_sem=recv,
            device_id=device, device_id_type=pl.DeviceIdType.MESH,
        )

    def own(hd, kv):
        return kvbuf.at[kv, 0, :, hd * HD:(hd + 1) * HD]

    def kv_copy(hd, slot, kv):
        forward = slot < 4 or (slot == 4 and kv == 0)
        if forward:
            src = own(hd, kv) if slot == 1 else win.at[hd, slot - 2, kv]
            device = along(1)
        elif slot == 8:
            src, device = own(hd, kv), along(ROW)
        else:
            src, device = win.at[hd, slot, kv], along(-1)
        return remote(src, win.at[hd, slot - 1, kv], kv_send.at[hd, slot - 1, kv],
                      kv_recv.at[hd, slot - 1, kv], device)

    def start_kv(hd):
        for kv in range(2):
            kv_copy(hd, 1, kv).start()
            kv_copy(hd, 8, kv).start()

    load_kv.wait()

    half, part = x // 2, lax.rem(x, 2)
    sign = 2 * low - 1
    w_targets = [
        (mod(high + sign, NH), 0, mod(-sign, NH)),
        (mod(high + sign, NH), 1, mod(-sign, NH)),
        (h_far, 1 - low, 2),
    ]
    w_copies = []
    for n, (h, l, k) in enumerate(w_targets):
        for c in range(NC):
            cols = pl.ds(pl.multiple_of((h * NC + c) * FEAT, FEAT), FEAT)
            w_copies.append(remote(
                w_hbm.at[half, part, :, cols], panel.at[k, half, core, part],
                wy_send.at[n, c], wy_recv, at_high(h, l, c),
            ))
    other = high * NC + (1 - core)
    w_sib = remote(
        w_hbm.at[:, :, :, pl.ds(pl.multiple_of(other * FEAT, FEAT), FEAT)],
        panel.at[0, :, core], ws_send, ws_recv, sibling,
    )
    w_sib.start()

    def w_stage_0():
        for copy in w_copies:
            copy.start()


    def w_quarter(by):
        xx = mod(x + by, NX)
        return panel.at[1:4, xx // 2, :, lax.rem(xx, 2)]

    def w_half(by, c):
        xx = mod(x + by, NX)
        return panel.at[1:4, xx // 2, c, lax.rem(xx, 2)]

    def await_bytes(ref, sem):
        pltpu.make_async_copy(ref, ref, sem).wait()

    wx_copies = [
        remote(w_quarter(0), w_quarter(0), wx_send.at[0], wx_recv.at[0], at_x(1)),
        remote(w_quarter(0), w_quarter(0), wx_send.at[1], wx_recv.at[1], at_x(-1)),
        remote(w_half(-1, 0), w_half(-1, 0), wx_send.at[2], wx_recv.at[2], at_x(1)),
        remote(w_half(1, 1), w_half(1, 1), wx_send.at[3], wx_recv.at[3], at_x(-1)),
    ]

    def w_stage_1():
        await_bytes(w_quarter(0), wy_recv)
        wx_copies[0].start()
        wx_copies[1].start()

    def w_stage_2():
        await_bytes(w_quarter(-1), wx_recv.at[0])
        wx_copies[2].start()
        await_bytes(w_quarter(1), wx_recv.at[1])
        wx_copies[3].start()

    def attend(hd, copy, chunks, first):
        q = qbuf[copy, :, hd * HD:(hd + 1) * HD]
        scores = []
        for keys, _, slot in chunks:
            s = lax.dot_general(
                q, keys, (((1,), (1,)), ((), ())), preferred_element_type=jnp.float32
            )
            s = s.reshape(BLOCKS, BLK // 8, 8, TOK) + bias[copy, slot][:, None]
            scores.append(s.reshape(TOK, TOK))
        best = scores[0]
        for s in scores[1:]:
            best = jnp.maximum(best, s)
        best = jnp.max(best, axis=1, keepdims=True)
        if first:
            new_top = jnp.broadcast_to(best, (TOK, HD))
        else:
            old_top = top[hd, copy]
            new_top = jnp.maximum(old_top, best)
        wide = jnp.concatenate([new_top, new_top], axis=1)
        gained = None
        for s, (_, values, _) in zip(scores, chunks):
            p = jnp.exp2((s - wide) * EXP_SCALE).astype(jnp.bfloat16)
            term = jnp.dot(
                p, jnp.concatenate([values, ones], axis=1), preferred_element_type=jnp.float32
            )
            gained = term if gained is None else gained + term
        if not first:
            fade = jnp.exp2((old_top - new_top) * EXP_SCALE)
            gained = gained + acc[hd, copy] * jnp.concatenate([fade, fade], axis=1)
        acc[hd, copy] = gained
        top[hd, copy] = new_top

    def finish(hd, copy):
        both = acc[hd, copy]
        att[hd, copy, 0, core] = (both[:, :HD] / both[:, HD:]).astype(jnp.bfloat16)

    def ag_up(hd, copy):
        return remote(att.at[hd, copy, 0, core], att.at[hd, copy, 3, core],
                      ag_send.at[hd, copy, 0], ag_recv.at[hd, copy, 2], at_high(h_up, low, core))

    def ag_down(hd, copy):
        return remote(att.at[hd, copy, 0, core], att.at[hd, copy, 1, core],
                      ag_send.at[hd, copy, 1], ag_recv.at[hd, copy, 0], at_high(h_down, low, core))

    def ag_far(hd, copy):
        slot = 3 if copy == 0 else 1
        to = h_up if copy == 0 else h_down
        return remote(att.at[hd, copy, slot, core], att.at[hd, copy, 2, core],
                      ag_send.at[hd, copy, 2], ag_recv.at[hd, copy, 1], at_high(to, low, core))

    def ag_sib(hd, copy, slot):
        return remote(att.at[hd, copy, slot, core], att.at[hd, copy, slot, core],
                      sib_send.at[hd, copy, slot], sib_recv.at[hd, copy, slot], sibling)

    def gather_start(hd, copy):
        ag_up(hd, copy).start()
        ag_down(hd, copy).start()
        ag_sib(hd, copy, 0).start()

    def gather_near(hd):
        for copy in range(2):
            order = (3, 1) if copy == 0 else (1, 3)
            for slot in order:
                if slot == 3:
                    ag_up(hd, copy).wait_recv()
                else:
                    ag_down(hd, copy).wait_recv()
                if slot == order[0]:
                    ag_far(hd, copy).start()
                ag_sib(hd, copy, slot).start()

    def gather_far(hd):
        for copy in range(2):
            ag_far(hd, copy).wait_recv()
            ag_sib(hd, copy, 2).start()

    def own_step(hd):
        keys, values = own(hd, 0)[...], own(hd, 1)[...]
        late_keys = kvbuf[0, 1, :, hd * HD:(hd + 1) * HD]
        late_values = kvbuf[1, 1, :, hd * HD:(hd + 1) * HD]
        attend(hd, 0, [(keys, values, 0)], True)
        attend(hd, 1, [(keys, values, 0), (late_keys, late_values, 9)], True)

    def pair_compute(hd, near, far, copy):
        chunks = [(win[hd, s - 1, 0], win[hd, s - 1, 1], s) for s in (near, far)]
        attend(hd, copy, chunks, False)

    def kv_step(hd, step):
        for kv in range(2):
            kv_copy(hd, 9 - step, kv).wait_recv()
            if step < 4 or kv == 1:
                kv_copy(hd, 8 - step, kv).start()
        for kv in range(2):
            kv_copy(hd, step, kv).wait_recv()
            if step < 3 or (step == 3 and kv == 0):
                kv_copy(hd, step + 1, kv).start()

    start_kv(0)
    start_kv(1)
    w_stage_0()

    lane_block = lax.broadcasted_iota(jnp.int32, (8, TOK), 1) // BLK
    for slot in range(9):
        here = ctx >= slot
        for a in range(BLOCKS):
            clean = jnp.zeros((8, TOK), jnp.int32)
            noisy = jnp.zeros((8, TOK), jnp.int32)
            for b in range(BLOCKS):
                gap = 4 * slot + a - b
                is_b = lane_block == b
                if 0 <= gap < WINB:
                    clean = jnp.where(is_b, 1, clean)
                if 1 <= gap <= WINB:
                    noisy = jnp.where(is_b, mask_ref[a, gap - 1], noisy)
            present = jnp.where(here, 1, 0)
            bias[0, slot, a] = jnp.where(clean * present == 1, 0.0, NEG)
            bias[1, slot, a] = jnp.where(noisy * present == 1, 0.0, NEG)
    for a in range(BLOCKS):
        bias[1, 9, a] = jnp.where(lane_block == a, 0.0, NEG)

    ones = jnp.ones((TOK, HD), jnp.bfloat16)

    load_q.wait()

    def compute_step(hd, step):
        for copy in range(2):
            pair_compute(hd, step, 9 - step, copy)
            if step == 4:
                finish(hd, copy)
                gather_start(hd, copy)

    def project(hd, copy, spots):
        rows = jnp.concatenate(
            [att[hd, copy, k, c] for k in spots for c in range(NC)], axis=1
        )
        weight = jnp.concatenate(
            [panel[k, hd].reshape(NC * HD, FEAT) for k in spots], axis=0
        )
        return jnp.dot(rows, weight, preferred_element_type=jnp.float32)

    def project_near():
        load_w.wait()
        await_bytes(panel.at[0, :, 1 - core], ws_recv)
        await_bytes(w_half(2, 0), wx_recv.at[2])
        await_bytes(w_half(2, 1), wx_recv.at[3])
        for hd in range(HEADS):
            for copy in range(2):
                for k in (0, 3, 1):
                    ag_sib(hd, copy, k).wait_recv()
                term = project(hd, copy, (0, 3, 1))
                total[copy] = term if hd == 0 else total[copy] + term

    for hd in range(HEADS):
        own_step(hd)
    for step in range(1, 5):
        for hd in range(HEADS):
            kv_step(hd, step)
            compute_step(hd, step)
        if step == 2:
            w_stage_1()
    gather_near(0)
    w_stage_2()
    gather_near(1)
    gather_far(0)
    project_near()
    gather_far(1)
    for copy in range(2):
        for hd in range(HEADS):
            ag_sib(hd, copy, 2).wait_recv()
        rows = jnp.concatenate(
            [att[hd, copy, 2, c] for hd in range(HEADS) for c in range(NC)], axis=1
        )
        weight = panel[2].reshape(HEADS * NC * HD, FEAT)
        term = jnp.dot(rows, weight, preferred_element_type=jnp.float32)
        out_ref[copy] = (total[copy] + term).astype(jnp.bfloat16)

    for hd in range(HEADS):
        for slot in range(1, 9):
            for kv in range(2):
                kv_copy(hd, slot, kv).wait_send()
        for copy in range(2):
            ag_up(hd, copy).wait_send()
            ag_down(hd, copy).wait_send()
            ag_far(hd, copy).wait_send()
            for slot in range(4):
                ag_sib(hd, copy, slot).wait_send()
    for copy in w_copies:
        copy.wait_send()
    w_sib.wait_send()
    for copy in wx_copies:
        copy.wait_send()


def on_device(queries, keys_values, block_mask, out_weight):
    weight = out_weight.reshape(HEADS, 2, HD // 2, out_weight.shape[1])
    dma = pltpu.SemaphoreType.DMA
    return pl.pallas_call(
        kernel,
        out_shape=jax.ShapeDtypeStruct((2, TOK, FEAT), jnp.bfloat16),
        in_specs=[
            pl.BlockSpec(memory_space=pltpu.SMEM),
            pl.BlockSpec(memory_space=pltpu.HBM),
            pl.BlockSpec(memory_space=pltpu.HBM),
            pl.BlockSpec(memory_space=pltpu.HBM),
        ],
        out_specs=pl.BlockSpec(memory_space=pltpu.VMEM),
        scratch_shapes=[
            pltpu.VMEM((2, TOK, HEADS * HD), jnp.bfloat16),
            pltpu.VMEM((2, 2, TOK, HEADS * HD), jnp.bfloat16),
            pltpu.VMEM((HEADS, 8, 2, TOK, HD), jnp.bfloat16),
            pltpu.VMEM((2, 10, BLOCKS, 8, TOK), jnp.float32),
            pltpu.VMEM((HEADS, 2, TOK, HD), jnp.float32),
            pltpu.VMEM((HEADS, 2, TOK, 2 * HD), jnp.float32),
            pltpu.VMEM((HEADS, 2, NH, NC, TOK, HD), jnp.bfloat16),
            pltpu.VMEM((NH, HEADS, NC, 2, HD // 2, FEAT), jnp.bfloat16),
            pltpu.VMEM((2, TOK, FEAT), jnp.float32),
            dma((3,)),
            dma((HEADS, 8, 2)),
            dma((HEADS, 8, 2)),
            dma((HEADS, 2, 3)),
            dma((HEADS, 2, 3)),
            dma((HEADS, 2, 4)),
            dma((HEADS, 2, 4)),
            dma((3, NC)),
            dma,
            dma,
            dma,
            dma((4,)),
            dma((4,)),
        ],
        compiler_params=pltpu.CompilerParams(
            collective_id=0, has_side_effects=True, vmem_limit_bytes=62 * 1024 * 1024
        ),
    )(block_mask, queries, keys_values, weight)


def solution(mesh):
    in_specs = (
        P(None, "ctx", "fsdp"),
        P(None, None, "ctx", "fsdp"),
        P("ctx", None),
        P("fsdp", None),
    )
    out_specs = P(None, "ctx", "fsdp")
    return jax.shard_map(
        on_device, mesh=mesh, in_specs=in_specs, out_specs=out_specs, check_vma=False
    )
```

time: 87.4 us -> 77.8 us (0.89)
  Pallas kernels: 82.1 us -> 75.8 us
  local copies, waits for them, and re-layouts: 5.06 us -> 1.87 us
    pallas_call x1, Pallas kernels: 82.1 us -> 75.8 us  [on_device(): pl.pallas_call(kernel, out_shape=jax.ShapeDtypeStruct((2, TOK, FEAT), jnp...]
    unnamed x9 -> x1, local copies, waits for them, and re-layouts: 5.06 us -> 1.87 us
where the time goes in v2:
time: 77.8 us; the launch traced here: 77.6 us
  Pallas kernels  75.8 us (97%)
  local copies, waits for them, and re-layouts  1.87 us (2%)
    pallas_call x1, Pallas kernels, on_device(): pl.pallas_call(kernel, out_shape=jax.ShapeDtypeStruct((2, TOK, FEAT), jnp...  75.8 us
    unnamed x1, local copies, waits for them, and re-layouts  1.87 us

profile of v2, /device:TPU:1, one launch (start us, length us, event | category | flops | bytes accessed | tf_op | source)
XLA Modules:
  0.0 77.6 jit_solution(4113275811600764546)
XLA Ops:
  0.0 75.8 %shard_map.46 = bf16[2,256,512]{2,1,0:T(8,128)(2,1)} custom-call(s32[4,32]{1,0:T(4,128)} %mask_ref.1, bf16[2,256,256]{2,1,0:T(8,128)(2,1)} %q_hbm.1, bf16[2,2,256,256]{3,2,1,0:T(8,128)(2,1)} %kv_hbm.1, bf16[2,2,64,4096]{3,2,1,0:T(8,128)(2,1)} %bitcast.1), custom_call_target="tpu_custom_call" | custom-call | tf_op jit(solution)/shard_map/pallas_call | solution.py:356
  75.8 1.9 %copy.6 = bf16[2,256,512]{2,1,0:T(8,128)(2,1)} copy(bf16[2,256,512]{2,1,0:T(8,128)(2,1)} %shard_map.46) | data formatting | bytes 1048576

commit v3 on v2

--- a/solution.py
+++ b/solution.py
@@ -19,6 +19,7 @@
 HEADS = 2
 FEAT = 512
 NEG = -1e30
+PAIR_STEP, RING_STEP = 1, 2
 EXP_SCALE = math.log2(math.e) / math.sqrt(HD)
 
 
@@ -30,7 +31,7 @@
     mask_ref, q_hbm, kv_hbm, w_hbm, out_ref,
     qbuf, kvbuf, win, bias, top, acc, att, panel, total,
     local_sem, kv_send, kv_recv, ag_send, ag_recv, sib_send, sib_recv,
-    wy_send, wy_recv, ws_send, ws_recv, wx_send, wx_recv,
+    wy_send, wy_recv, wp_send, wp_recv, ws_send, ws_recv, wx_send, wx_recv,
 ):
     ctx = lax.axis_index("ctx")
     fsdp = lax.axis_index("fsdp")
@@ -55,7 +56,7 @@
     load_kv = pltpu.make_async_copy(kv_hbm, kvbuf, local_sem.at[0])
     load_q = pltpu.make_async_copy(q_hbm, qbuf, local_sem.at[1])
     load_w = pltpu.make_async_copy(
-        w_hbm.at[:, :, :, pl.ds(pl.multiple_of(fsdp * FEAT, FEAT), FEAT)],
+        w_hbm.at[:, :, :, :, pl.ds(pl.multiple_of(fsdp * FEAT, FEAT), FEAT)],
         panel.at[0, :, core],
         local_sem.at[2],
     )
@@ -101,7 +102,7 @@
 
     load_kv.wait()
 
-    half, part = x // 2, lax.rem(x, 2)
+    half, part, odd = x // 2, lax.rem(x, 2), lax.rem(z, 2)
     sign = 2 * low - 1
     w_targets = [
         (mod(high + sign, NH), 0, mod(-sign, NH)),
@@ -113,12 +114,12 @@
         for c in range(NC):
             cols = pl.ds(pl.multiple_of((h * NC + c) * FEAT, FEAT), FEAT)
             w_copies.append(remote(
-                w_hbm.at[half, part, :, cols], panel.at[k, half, core, part],
+                w_hbm.at[half, part, odd, :, cols], panel.at[k, half, core, part, odd],
                 wy_send.at[n, c], wy_recv, at_high(h, l, c),
             ))
     other = high * NC + (1 - core)
     w_sib = remote(
-        w_hbm.at[:, :, :, pl.ds(pl.multiple_of(other * FEAT, FEAT), FEAT)],
+        w_hbm.at[:, :, :, :, pl.ds(pl.multiple_of(other * FEAT, FEAT), FEAT)],
         panel.at[0, :, core], ws_send, ws_recv, sibling,
     )
     w_sib.start()
@@ -146,12 +147,19 @@
         remote(w_half(1, 1), w_half(1, 1), wx_send.at[3], wx_recv.at[3], at_x(-1)),
     ]
 
+    share = panel.at[1:4, half, :, part, odd]
+    w_pair = remote(share, share, wp_send, wp_recv, along(1 - 2 * odd))
+
     def w_stage_1():
-        await_bytes(w_quarter(0), wy_recv)
+        await_bytes(share, wy_recv)
+        w_pair.start()
+
+    def w_stage_2():
+        w_pair.wait_recv()
         wx_copies[0].start()
         wx_copies[1].start()
 
-    def w_stage_2():
+    def w_stage_3():
         await_bytes(w_quarter(-1), wx_recv.at[0])
         wx_copies[2].start()
         await_bytes(w_quarter(1), wx_recv.at[1])
@@ -315,10 +323,12 @@
         for hd in range(HEADS):
             kv_step(hd, step)
             compute_step(hd, step)
-        if step == 2:
+        if step == PAIR_STEP:
             w_stage_1()
+        if step == RING_STEP:
+            w_stage_2()
     gather_near(0)
-    w_stage_2()
+    w_stage_3()
     gather_near(1)
     gather_far(0)
     project_near()
@@ -346,12 +356,13 @@
     for copy in w_copies:
         copy.wait_send()
     w_sib.wait_send()
+    w_pair.wait_send()
     for copy in wx_copies:
         copy.wait_send()
 
 
 def on_device(queries, keys_values, block_mask, out_weight):
-    weight = out_weight.reshape(HEADS, 2, HD // 2, out_weight.shape[1])
+    weight = out_weight.reshape(HEADS, 2, 2, HD // 4, out_weight.shape[1])
     dma = pltpu.SemaphoreType.DMA
     return pl.pallas_call(
         kernel,
@@ -371,7 +382,7 @@
             pltpu.VMEM((HEADS, 2, TOK, HD), jnp.float32),
             pltpu.VMEM((HEADS, 2, TOK, 2 * HD), jnp.float32),
             pltpu.VMEM((HEADS, 2, NH, NC, TOK, HD), jnp.bfloat16),
-            pltpu.VMEM((NH, HEADS, NC, 2, HD // 2, FEAT), jnp.bfloat16),
+            pltpu.VMEM((NH, HEADS, NC, 2, 2, HD // 4, FEAT), jnp.bfloat16),
             pltpu.VMEM((2, TOK, FEAT), jnp.float32),
             dma((3,)),
             dma((HEADS, 8, 2)),
@@ -384,6 +395,8 @@
             dma,
             dma,
             dma,
+            dma,
+            dma,
             dma((4,)),
             dma((4,)),
         ],

time: 77.8 us -> 74.2 us (0.954)
  Pallas kernels: 75.8 us -> 72.1 us
    pallas_call x1, Pallas kernels: 75.8 us -> 72.1 us  [on_device(): pl.pallas_call(kernel, out_shape=jax.ShapeDtypeStruct((2, TOK, FEAT), jnp...]
where the time goes in v3:
time: 74.2 us; the launch traced here: 74 us
  Pallas kernels  72.1 us (97%)
  local copies, waits for them, and re-layouts  1.87 us (3%)
    pallas_call x1, Pallas kernels, on_device(): pl.pallas_call(kernel, out_shape=jax.ShapeDtypeStruct((2, TOK, FEAT), jnp...  72.1 us
    unnamed x1, local copies, waits for them, and re-layouts  1.87 us

profile of v3, /device:TPU:1, one launch (start us, length us, event | category | flops | bytes accessed | tf_op | source)
XLA Modules:
  0.0 74.0 jit_solution(13482912104587724870)
XLA Ops:
  0.0 72.1 %shard_map.46 = bf16[2,256,512]{2,1,0:T(8,128)(2,1)} custom-call(s32[4,32]{1,0:T(4,128)} %mask_ref.1, bf16[2,256,256]{2,1,0:T(8,128)(2,1)} %q_hbm.1, bf16[2,2,256,256]{3,2,1,0:T(8,128)(2,1)} %kv_hbm.1, bf16[2,2,2,32,4096]{4,3,2,1,0:T(8,128)(2,1)} %bitcast.1), custom_call_target="tpu_custom_call" | custom-call | tf_op jit(solution)/shard_map/pallas_call | solution.py:367
  72.2 1.9 %copy.6 = bf16[2,256,512]{2,1,0:T(8,128)(2,1)} copy(bf16[2,256,512]{2,1,0:T(8,128)(2,1)} %shard_map.46) | data formatting | bytes 1048576

commit v4 on v3

--- a/solution.py
+++ b/solution.py
@@ -127,7 +127,6 @@
     def w_stage_0():
         for copy in w_copies:
             copy.start()
-
 
     def w_quarter(by):
         xx = mod(x + by, NX)
@@ -322,7 +321,11 @@
     for step in range(1, 5):
         for hd in range(HEADS):
             kv_step(hd, step)
-            compute_step(hd, step)
+            if step == 4:
+                compute_step(hd, step)
+        if step < 4:
+            for hd in range(HEADS):
+                compute_step(hd, step)
         if step == PAIR_STEP:
             w_stage_1()
         if step == RING_STEP:
@@ -332,6 +335,22 @@
     gather_near(1)
     gather_far(0)
     project_near()
+
+    for hd in range(HEADS):
+        for slot in range(1, 9):
+            for kv in range(2):
+                kv_copy(hd, slot, kv).wait_send()
+        for copy in range(2):
+            ag_up(hd, copy).wait_send()
+            ag_down(hd, copy).wait_send()
+            for slot in (0, 1, 3):
+                ag_sib(hd, copy, slot).wait_send()
+            if hd == 0:
+                ag_far(hd, copy).wait_send()
+                ag_sib(hd, copy, 2).wait_send()
+    for copy in w_copies + wx_copies + [w_sib, w_pair]:
+        copy.wait_send()
+
     gather_far(1)
     for copy in range(2):
         for hd in range(HEADS):
@@ -343,22 +362,9 @@
         term = jnp.dot(rows, weight, preferred_element_type=jnp.float32)
         out_ref[copy] = (total[copy] + term).astype(jnp.bfloat16)
 
-    for hd in range(HEADS):
-        for slot in range(1, 9):
-            for kv in range(2):
-                kv_copy(hd, slot, kv).wait_send()
-        for copy in range(2):
-            ag_up(hd, copy).wait_send()
-            ag_down(hd, copy).wait_send()
-            ag_far(hd, copy).wait_send()
-            for slot in range(4):
-                ag_sib(hd, copy, slot).wait_send()
-    for copy in w_copies:
-        copy.wait_send()
-    w_sib.wait_send()
-    w_pair.wait_send()
-    for copy in wx_copies:
-        copy.wait_send()
+    for copy in range(2):
+        ag_far(1, copy).wait_send()
+        ag_sib(1, copy, 2).wait_send()
 
 
 def on_device(queries, keys_values, block_mask, out_weight):

time: 74.2 us -> 74.3 us (level)
  no operation moved by 1% of the time
where the time goes in v4:
time: 74.3 us; the launch traced here: 74.1 us
  Pallas kernels  72.2 us (97%)
  local copies, waits for them, and re-layouts  1.87 us (3%)
    pallas_call x1, Pallas kernels, on_device(): pl.pallas_call(kernel, out_shape=jax.ShapeDtypeStruct((2, TOK, FEAT), jnp...  72.2 us
    unnamed x1, local copies, waits for them, and re-layouts  1.87 us

profile of v4, /device:TPU:1, one launch (start us, length us, event | category | flops | bytes accessed | tf_op | source)
XLA Modules:
  0.0 74.1 jit_solution(12765914079287527721)
XLA Ops:
  0.0 72.2 %shard_map.46 = bf16[2,256,512]{2,1,0:T(8,128)(2,1)} custom-call(s32[4,32]{1,0:T(4,128)} %mask_ref.1, bf16[2,256,256]{2,1,0:T(8,128)(2,1)} %q_hbm.1, bf16[2,2,256,256]{3,2,1,0:T(8,128)(2,1)} %kv_hbm.1, bf16[2,2,2,32,4096]{4,3,2,1,0:T(8,128)(2,1)} %bitcast.1), custom_call_target="tpu_custom_call" | custom-call | tf_op jit(solution)/shard_map/pallas_call | solution.py:373
  72.2 1.9 %copy.6 = bf16[2,256,512]{2,1,0:T(8,128)(2,1)} copy(bf16[2,256,512]{2,1,0:T(8,128)(2,1)} %shard_map.46) | data formatting | bytes 1048576
